TPU v7x, 256 devices: a whole 4x4x8 slice. The times are simulated.
256 devices in a mesh: dp: 32 (over z, y_hi, core), fsdp: 8 (over y_lo, x).
Axes of the slice: x: 4, y: 4 (y_hi: 2, y_lo: 2; y = y_hi * 2 + y_lo), z: 8, core: 2. Of those that a mesh axis runs over, the one named last changes fastest.
Arguments:
- hidden: bfloat16 [131072, 1152], P(('dp', 'fsdp')), may hold values from -6 to 6
- text_ids: int32 [8192, 16], P(('dp', 'fsdp')), may hold values from 0 to 31999, as said below
- ln_gain: float32 [1152], replicated, may hold values from 0.5 to 1.5
- ln_bias: float32 [1152], replicated, may hold values from -2 to 2
- fc1_weight: bfloat16 [1152, 4304], P(None, 'fsdp'), may hold values from -0.1875 to 0.1875
- fc1_bias: float32 [4304], replicated, may hold values from -3 to 3
- fc2_weight: bfloat16 [4304, 1152], P('fsdp'), may hold values from -0.09375 to 0.09375
- fc2_bias: float32 [1152], replicated, may hold values from -3 to 3
- final_gain: float32 [1152], replicated, may hold values from 0.5 to 1.5
- final_bias: float32 [1152], replicated, may hold values from -0.2 to 0.2
- head_weight: bfloat16 [1152, 1152], replicated, may hold values from -0.1875 to 0.1875
- head_bias: float32 [1152], replicated, may hold values from -0.3 to 0.3
- image_emb: bfloat16 [8192, 1152], P(('dp', 'fsdp')), may hold values from -6 to 6
- teacher_logits: bfloat16 [8192, 12, 256], P('dp', None, 'fsdp'), may hold values from -12 to 12
- logit_scale: float32 [1], replicated, may hold values from 4 to 16
- logit_bias: float32 [1], replicated, may hold values from -3 to 0
Outputs:
- image_grad: float32 [8192, 1152], P(('dp', 'fsdp'))
Inputs may be any that keep to these rules, and one draw needn't show every extreme that they name: `text_ids`: 0 marks padding after a text's end; every text has at least one token and the tokens of a text come first.
All inputs are finite; a program needn't handle non-finite values.
Results may differ from a plain program's by a relative error of at most 0.0018.
Values may be sent and summed in bfloat16 or wider, within the bound.
No kernel may reach another device: no remote copies, remote signals or barrier semaphores. Data moves between devices by JAX's collectives and lax.ppermute only.
A program may use at most 128 MiB of HBM per device.

v0:
```python
import jax
import jax.numpy as jnp
from jax import lax
from jax.sharding import PartitionSpec as P


def from_everyone(array, axis):
    copies = jnp.broadcast_to(array, (lax.axis_size(axis), *array.shape))
    return lax.all_to_all(copies, axis, split_axis=0, concat_axis=0, tiled=True)


def joined_along(parts, dim):
    parts = jnp.moveaxis(parts, 0, dim)
    dims = parts.shape
    return parts.reshape(*dims[:dim], dims[dim] * dims[dim + 1], *dims[dim + 2 :])


def gather_directly(array, axis, dim):
    parts = from_everyone(array, axis)
    return joined_along(parts, dim)


def from_behind(array, axis, by):
    count = lax.axis_size(axis)
    return lax.ppermute(array, axis, [(i, (i + by) % count) for i in range(count)])


def layer_norm(values, gain, shift):
    centre = jnp.mean(values, axis=-1, keepdims=True)
    spread = jnp.mean((values - centre) ** 2, axis=-1, keepdims=True)
    return (values - centre) * lax.rsqrt(spread + 1e-06) * gain + shift


def on_device(
    hidden,
    text_ids,
    ln_gain,
    ln_bias,
    fc1_weight,
    fc1_bias,
    fc2_weight,
    fc2_bias,
    final_gain,
    final_bias,
    head_weight,
    head_bias,
    image_emb,
    teacher_logits,
    logit_scale,
    logit_bias,
):
    width = hidden.shape[1]
    texts_here, seq_len = text_ids.shape
    window = teacher_logits.shape[1]
    flat = hidden.astype(jnp.float32)
    normed = layer_norm(flat, ln_gain, ln_bias).astype(jnp.bfloat16)
    pre = (
        jnp.dot(
            normed,
            lax.all_gather(fc1_weight, "fsdp", axis=1, tiled=True),
            preferred_element_type=jnp.float32,
        )
        + fc1_bias
    )
    act = jax.nn.gelu(pre, approximate=True).astype(jnp.bfloat16)
    mixed = jnp.dot(
        act,
        lax.all_gather(fc2_weight, "fsdp", axis=0, tiled=True),
        preferred_element_type=jnp.float32,
    )
    out = flat + mixed + fc2_bias
    final = layer_norm(out, final_gain, final_bias).reshape(texts_here, seq_len, width)
    keep = (text_ids != 0).astype(jnp.float32)
    pooled = jnp.sum(final * keep[:, :, None], axis=1) / jnp.sum(keep, axis=1)[:, None]
    emb = (
        jnp.dot(pooled.astype(jnp.bfloat16), head_weight, preferred_element_type=jnp.float32)
        + head_bias
    )
    text_unit = (emb * lax.rsqrt(jnp.sum(emb * emb, axis=-1, keepdims=True) + 1e-06)).astype(
        jnp.bfloat16
    )
    group_units = gather_directly(text_unit, "fsdp", 0)
    images = image_emb.astype(jnp.float32)
    image_unit = (
        images * lax.rsqrt(jnp.sum(images * images, axis=-1, keepdims=True) + 1e-06)
    ).astype(jnp.bfloat16)
    scale = logit_scale[0]
    offset = logit_bias[0]

    def pair_term(units, pictures, tile):
        score = (
            scale
            * lax.dot_general(
                units, pictures, (((1,), (1,)), ((), ())), preferred_element_type=jnp.float32
            )
            + offset
        )
        weight = (jax.nn.sigmoid(score) - jax.nn.sigmoid(tile.astype(jnp.float32))).astype(
            jnp.bfloat16
        )
        return lax.dot_general(
            weight, units, (((0,), (0,)), ((), ())), preferred_element_type=jnp.float32
        )

    start_grad = jnp.zeros(image_unit.shape, jnp.float32)

    def turn_images(step, carry):
        pictures, total = carry
        tile = lax.dynamic_index_in_dim(teacher_logits, step, 1, keepdims=False)
        total = total + pair_term(group_units, pictures, tile)
        pictures, total = (
            from_behind(pictures.astype(jnp.float32), "dp", -1).astype(pictures.dtype),
            from_behind(total, "dp", -1),
        )
        return (pictures, total)

    pictures, total = lax.fori_loop(0, window - 1, turn_images, (image_unit, start_grad))
    total = total + pair_term(group_units, pictures, teacher_logits[:, window - 1, :])
    total = from_behind(total, "dp", window - 1)
    return scale * total


def solution(mesh):
    placed = (
        P(("dp", "fsdp"), None),
        P(("dp", "fsdp"), None),
        P(),
        P(),
        P(None, "fsdp"),
        P(),
        P("fsdp", None),
        P(),
        P(),
        P(),
        P(),
        P(),
        P(("dp", "fsdp"), None),
        P("dp", None, "fsdp"),
        P(),
        P(),
    )
    return jax.shard_map(
        on_device, mesh=mesh, in_specs=placed, out_specs=P(("dp", "fsdp"), None), check_vma=False
    )
```

profile of v0, /device:TPU:1, one launch (start us, length us, event | category | flops | bytes accessed | tf_op | source)
XLA Modules:
  0.0 442.1 jit_solution(9942454543745646307)
XLA Ops:
  11.5 111.0 %all-gather.5.cloned.1.call-done = bf16[8,538,1152]{2,1,0:T(8,128)(2,1)} async-done(((bf16[1,538,1152]{2,1,0:T(8,128)(2,1)}), bf16[8,538,1152]{2,1,0:T(8,128)(2,1)}) %all-gather.5.cloned.1.call-update) | async-done | bytes 9916432 | tf_op jit(solution)/shard_map/all_gather | solution.py:60
  122.5 11.8 %reshape.68 = bf16[4304,1152]{1,0:T(8,128)(2,1)} reshape(bf16[8,538,1152]{2,1,0:T(8,128)(2,1)} %all-gather.5.cloned.1.call-done) | data formatting | bytes 19832832
  134.4 98.5 %all-gather.7.cloned.1.call-done = bf16[8,538,1152]{2,1,0:T(8,128)(2,1)} async-done(((bf16[1,538,1152]{2,1,0:T(8,128)(2,1)}), bf16[8,538,1152]{2,1,0:T(8,128)(2,1)}) %all-gather.7.cloned.1.call-update) | async-done | bytes 9916432 | tf_op jit(solution)/shard_map/all_gather | solution.py:68
  232.9 11.9 %reshape.70 = bf16[4304,1152]{1,0:T(8,128)(2,1)} reshape(bf16[8,538,1152]{2,1,0:T(8,128)(2,1)} %all-gather.7.cloned.1.call-done) | data formatting | bytes 19832832
  244.8 23.1 %fusion.72 = (f32[512]{0:T(512)S(1)}, f32[512,1152]{1,0:T(8,128)}) fusion(f32[1152]{0:T(1024)S(1)} %copy-done.8, bf16[4304,1152]{1,0:T(8,128)(2,1)} %reshape.70, bf16[4304,1152]{1,0:T(8,128)(2,1)} %reshape.68, f32[4304]{0:T(1024)S(1)} %copy-done.7, bf16[512,1152]{1,0:T(8,128)(2,1)} %param.18, f32[1152]{0:T(1024)S(1)} %copy-done.9, f32[1152]{0:T(1024)S(1)} %copy-done.10, ...), kind=kOutput, calls=%fused_computation.91 | convolution fusion | flops 10182344704 | bytes 23408960 | tf_op jit(solution)/shard_map/dot_general | solution.py:66
  272.9 3.5 all-to-all-start
  277.8 9.5 %all-to-all-done = bf16[8,32,1152]{2,1,0:T(8,128)(2,1)S(1)} async-done(((bf16[8,32,1152]{2,1,0:T(8,128)(2,1)}), bf16[8,32,1152]{2,1,0:T(8,128)(2,1)S(1)}, u32[]{:S(2)}, u32[]{:S(2)}) %all-to-all-start) | async-done | bytes 589856 | tf_op jit(solution)/shard_map/all_to_all | solution.py:9
  287.3 134.7 %while.15 = (s32[]{:T(128)}, bf16[32,1152]{1,0:T(8,128)(2,1)S(1)}, f32[32,1152]{1,0:T(8,128)S(1)}, f32[]{:T(128)}, bf16[256,1152]{1,0:T(8,128)(2,1)S(1)}, /*inde...) while((s32[]{:T(128)}, bf16[32,1152]{1,0:T(8,128)(2,1)S(1)}, f32[32,1152]{1,0:T(8,128)S(1)}, f32[]{:T(128)}, ...), condition=%wide.region_9.10_spmd, body=%wide.region_8.9_spmd.sunk | while | flops 37875712 | bytes 2598565 | solution.py:117
  287.4 3.3 convolution_add_fusion.4
  291.4 4.8 %collective-permute-start = (bf16[32,1152]{1,0:T(8,128)(2,1)S(1)}, bf16[32,1152]{1,0:T(8,128)(2,1)S(1)}, u32[]{:S(2)}, u32[]{:S(2)}) collective-permute-start(bf16[32,1152]{1,0:T(8,128)(2,1)S(1)} %copy.24), channel_id=1, source_target_pairs={{0,248},{8,0},{16,8},{24,16},{32,24},{40,32},{48,40},{56,48},{64,5... | collective-permute-start | bytes 221192 | tf_op jit(solution)/shard_map/while/body/eval_jaxpr/ppermute | solution.py:25
  297.7 3.3 convolution_add_fusion.4
  303.2 5.5 %collective-permute-start = (bf16[32,1152]{1,0:T(8,128)(2,1)S(1)}, bf16[32,1152]{1,0:T(8,128)(2,1)S(1)}, u32[]{:S(2)}, u32[]{:S(2)}) collective-permute-start(bf16[32,1152]{1,0:T(8,128)(2,1)S(1)} %copy.24), channel_id=1, source_target_pairs={{0,248},{8,0},{16,8},{24,16},{32,24},{40,32},{48,40},{56,48},{64,5... | collective-permute-start | bytes 221192 | tf_op jit(solution)/shard_map/while/body/eval_jaxpr/ppermute | solution.py:25
  309.7 3.3 convolution_add_fusion.4
  315.7 5.5 %collective-permute-start = (bf16[32,1152]{1,0:T(8,128)(2,1)S(1)}, bf16[32,1152]{1,0:T(8,128)(2,1)S(1)}, u32[]{:S(2)}, u32[]{:S(2)}) collective-permute-start(bf16[32,1152]{1,0:T(8,128)(2,1)S(1)} %copy.24), channel_id=1, source_target_pairs={{0,248},{8,0},{16,8},{24,16},{32,24},{40,32},{48,40},{56,48},{64,5... | collective-permute-start | bytes 221192 | tf_op jit(solution)/shard_map/while/body/eval_jaxpr/ppermute | solution.py:25
  322.1 3.3 convolution_add_fusion.4
  328.2 5.5 %collective-permute-start = (bf16[32,1152]{1,0:T(8,128)(2,1)S(1)}, bf16[32,1152]{1,0:T(8,128)(2,1)S(1)}, u32[]{:S(2)}, u32[]{:S(2)}) collective-permute-start(bf16[32,1152]{1,0:T(8,128)(2,1)S(1)} %copy.24), channel_id=1, source_target_pairs={{0,248},{8,0},{16,8},{24,16},{32,24},{40,32},{48,40},{56,48},{64,5... | collective-permute-start | bytes 221192 | tf_op jit(solution)/shard_map/while/body/eval_jaxpr/ppermute | solution.py:25
  340.7 5.5 %collective-permute-start = (bf16[32,1152]{1,0:T(8,128)(2,1)S(1)}, bf16[32,1152]{1,0:T(8,128)(2,1)S(1)}, u32[]{:S(2)}, u32[]{:S(2)}) collective-permute-start(bf16[32,1152]{1,0:T(8,128)(2,1)S(1)} %copy.24), channel_id=1, source_target_pairs={{0,248},{8,0},{16,8},{24,16},{32,24},{40,32},{48,40},{56,48},{64,5... | collective-permute-start | bytes 221192 | tf_op jit(solution)/shard_map/while/body/eval_jaxpr/ppermute | solution.py:25
  353.1 5.5 %collective-permute-start = (bf16[32,1152]{1,0:T(8,128)(2,1)S(1)}, bf16[32,1152]{1,0:T(8,128)(2,1)S(1)}, u32[]{:S(2)}, u32[]{:S(2)}) collective-permute-start(bf16[32,1152]{1,0:T(8,128)(2,1)S(1)} %copy.24), channel_id=1, source_target_pairs={{0,248},{8,0},{16,8},{24,16},{32,24},{40,32},{48,40},{56,48},{64,5... | collective-permute-start | bytes 221192 | tf_op jit(solution)/shard_map/while/body/eval_jaxpr/ppermute | solution.py:25
  365.6 5.5 %collective-permute-start = (bf16[32,1152]{1,0:T(8,128)(2,1)S(1)}, bf16[32,1152]{1,0:T(8,128)(2,1)S(1)}, u32[]{:S(2)}, u32[]{:S(2)}) collective-permute-start(bf16[32,1152]{1,0:T(8,128)(2,1)S(1)} %copy.24), channel_id=1, source_target_pairs={{0,248},{8,0},{16,8},{24,16},{32,24},{40,32},{48,40},{56,48},{64,5... | collective-permute-start | bytes 221192 | tf_op jit(solution)/shard_map/while/body/eval_jaxpr/ppermute | solution.py:25
  378.1 5.5 %collective-permute-start = (bf16[32,1152]{1,0:T(8,128)(2,1)S(1)}, bf16[32,1152]{1,0:T(8,128)(2,1)S(1)}, u32[]{:S(2)}, u32[]{:S(2)}) collective-permute-start(bf16[32,1152]{1,0:T(8,128)(2,1)S(1)} %copy.24), channel_id=1, source_target_pairs={{0,248},{8,0},{16,8},{24,16},{32,24},{40,32},{48,40},{56,48},{64,5... | collective-permute-start | bytes 221192 | tf_op jit(solution)/shard_map/while/body/eval_jaxpr/ppermute | solution.py:25
  390.6 5.5 %collective-permute-start = (bf16[32,1152]{1,0:T(8,128)(2,1)S(1)}, bf16[32,1152]{1,0:T(8,128)(2,1)S(1)}, u32[]{:S(2)}, u32[]{:S(2)}) collective-permute-start(bf16[32,1152]{1,0:T(8,128)(2,1)S(1)} %copy.24), channel_id=1, source_target_pairs={{0,248},{8,0},{16,8},{24,16},{32,24},{40,32},{48,40},{56,48},{64,5... | collective-permute-start | bytes 221192 | tf_op jit(solution)/shard_map/while/body/eval_jaxpr/ppermute | solution.py:25
  403.1 5.5 %collective-permute-start = (bf16[32,1152]{1,0:T(8,128)(2,1)S(1)}, bf16[32,1152]{1,0:T(8,128)(2,1)S(1)}, u32[]{:S(2)}, u32[]{:S(2)}) collective-permute-start(bf16[32,1152]{1,0:T(8,128)(2,1)S(1)} %copy.24), channel_id=1, source_target_pairs={{0,248},{8,0},{16,8},{24,16},{32,24},{40,32},{48,40},{56,48},{64,5... | collective-permute-start | bytes 221192 | tf_op jit(solution)/shard_map/while/body/eval_jaxpr/ppermute | solution.py:25
  415.6 5.5 %collective-permute-start = (bf16[32,1152]{1,0:T(8,128)(2,1)S(1)}, bf16[32,1152]{1,0:T(8,128)(2,1)S(1)}, u32[]{:S(2)}, u32[]{:S(2)}) collective-permute-start(bf16[32,1152]{1,0:T(8,128)(2,1)S(1)} %copy.24), channel_id=1, source_target_pairs={{0,248},{8,0},{16,8},{24,16},{32,24},{40,32},{48,40},{56,48},{64,5... | collective-permute-start | bytes 221192 | tf_op jit(solution)/shard_map/while/body/eval_jaxpr/ppermute | solution.py:25
  424.0 10.6 %collective-permute-done.2 = f32[32,1152]{1,0:T(8,128)S(1)} collective-permute-done((f32[32,1152]{1,0:T(8,128)}, f32[32,1152]{1,0:T(8,128)S(1)}, u32[]{:S(2)}, u32[]{:S(2)}) %collective-permute-start.2) | collective-permute-done | bytes 147488 | tf_op jit(solution)/shard_map/ppermute | solution.py:25
  (99 shorter events, 74.0 us)
Async XLA Ops:
  6.5 116.0 %all-gather.5.cloned.1.call-start = ((), (), s32[]{:S(2)}) async-start(), calls=%async_computation.1 | async-start | bytes 11280384 | tf_op jit(solution)/shard_map/all_gather | solution.py:60
  7.3 225.6 %all-gather.7.cloned.1.call-start = ((), (), s32[]{:S(2)}) async-start(), calls=%async_computation.2 | async-start | bytes 11280384 | tf_op jit(solution)/shard_map/all_gather | solution.py:68
  272.9 14.4 %all-to-all-start = ((bf16[8,32,1152]{2,1,0:T(8,128)(2,1)}), bf16[8,32,1152]{2,1,0:T(8,128)(2,1)S(1)}, u32[]{:S(2)}, u32[]{:S(2)}) async-start(bf16[8,32,1152]{2,1,0:T(8,128)(2,1)} %broadcast_in_dim.5), calls=%async_computation | async-start | bytes 1179648 | tf_op jit(solution)/shard_map/all_to_all | solution.py:9
  290.7 7.1 %collective-permute-start.1 = (f32[32,1152]{1,0:T(8,128)}, f32[32,1152]{1,0:T(8,128)S(1)}, u32[]{:S(2)}, u32[]{:S(2)}) collective-permute-start(f32[32,1152]{1,0:T(8,128)} %convolution_add_fusion.4), channel_id=1, source_target_pairs={{0,248},{8,0},{16,8},{24,16},{32,24},{40,32},{48,40},{56,48},{64,5... | collective-permute-start | bytes 442376 | tf_op jit(solution)/shard_map/while/body/eval_jaxpr/ppermute | solution.py:25
  301.0 8.6 %collective-permute-start.1 = (f32[32,1152]{1,0:T(8,128)}, f32[32,1152]{1,0:T(8,128)S(1)}, u32[]{:S(2)}, u32[]{:S(2)}) collective-permute-start(f32[32,1152]{1,0:T(8,128)} %convolution_add_fusion.4), channel_id=1, source_target_pairs={{0,248},{8,0},{16,8},{24,16},{32,24},{40,32},{48,40},{56,48},{64,5... | collective-permute-start | bytes 442376 | tf_op jit(solution)/shard_map/while/body/eval_jaxpr/ppermute | solution.py:25
  303.2 6.4 %collective-permute-start = (bf16[32,1152]{1,0:T(8,128)(2,1)S(1)}, bf16[32,1152]{1,0:T(8,128)(2,1)S(1)}, u32[]{:S(2)}, u32[]{:S(2)}) collective-permute-start(bf16[32,1152]{1,0:T(8,128)(2,1)S(1)} %copy.24), channel_id=1, source_target_pairs={{0,248},{8,0},{16,8},{24,16},{32,24},{40,32},{48,40},{56,48},{64,5... | collective-permute-start | bytes 221192 | tf_op jit(solution)/shard_map/while/body/eval_jaxpr/ppermute | solution.py:25
  312.9 9.2 %collective-permute-start.1 = (f32[32,1152]{1,0:T(8,128)}, f32[32,1152]{1,0:T(8,128)S(1)}, u32[]{:S(2)}, u32[]{:S(2)}) collective-permute-start(f32[32,1152]{1,0:T(8,128)} %convolution_add_fusion.4), channel_id=1, source_target_pairs={{0,248},{8,0},{16,8},{24,16},{32,24},{40,32},{48,40},{56,48},{64,5... | collective-permute-start | bytes 442376 | tf_op jit(solution)/shard_map/while/body/eval_jaxpr/ppermute | solution.py:25
  315.7 6.4 %collective-permute-start = (bf16[32,1152]{1,0:T(8,128)(2,1)S(1)}, bf16[32,1152]{1,0:T(8,128)(2,1)S(1)}, u32[]{:S(2)}, u32[]{:S(2)}) collective-permute-start(bf16[32,1152]{1,0:T(8,128)(2,1)S(1)} %copy.24), channel_id=1, source_target_pairs={{0,248},{8,0},{16,8},{24,16},{32,24},{40,32},{48,40},{56,48},{64,5... | collective-permute-start | bytes 221192 | tf_op jit(solution)/shard_map/while/body/eval_jaxpr/ppermute | solution.py:25
  325.4 9.2 %collective-permute-start.1 = (f32[32,1152]{1,0:T(8,128)}, f32[32,1152]{1,0:T(8,128)S(1)}, u32[]{:S(2)}, u32[]{:S(2)}) collective-permute-start(f32[32,1152]{1,0:T(8,128)} %convolution_add_fusion.4), channel_id=1, source_target_pairs={{0,248},{8,0},{16,8},{24,16},{32,24},{40,32},{48,40},{56,48},{64,5... | collective-permute-start | bytes 442376 | tf_op jit(solution)/shard_map/while/body/eval_jaxpr/ppermute | solution.py:25
  328.2 6.4 %collective-permute-start = (bf16[32,1152]{1,0:T(8,128)(2,1)S(1)}, bf16[32,1152]{1,0:T(8,128)(2,1)S(1)}, u32[]{:S(2)}, u32[]{:S(2)}) collective-permute-start(bf16[32,1152]{1,0:T(8,128)(2,1)S(1)} %copy.24), channel_id=1, source_target_pairs={{0,248},{8,0},{16,8},{24,16},{32,24},{40,32},{48,40},{56,48},{64,5... | collective-permute-start | bytes 221192 | tf_op jit(solution)/shard_map/while/body/eval_jaxpr/ppermute | solution.py:25
  337.9 9.2 %collective-permute-start.1 = (f32[32,1152]{1,0:T(8,128)}, f32[32,1152]{1,0:T(8,128)S(1)}, u32[]{:S(2)}, u32[]{:S(2)}) collective-permute-start(f32[32,1152]{1,0:T(8,128)} %convolution_add_fusion.4), channel_id=1, source_target_pairs={{0,248},{8,0},{16,8},{24,16},{32,24},{40,32},{48,40},{56,48},{64,5... | collective-permute-start | bytes 442376 | tf_op jit(solution)/shard_map/while/body/eval_jaxpr/ppermute | solution.py:25
  340.7 6.4 %collective-permute-start = (bf16[32,1152]{1,0:T(8,128)(2,1)S(1)}, bf16[32,1152]{1,0:T(8,128)(2,1)S(1)}, u32[]{:S(2)}, u32[]{:S(2)}) collective-permute-start(bf16[32,1152]{1,0:T(8,128)(2,1)S(1)} %copy.24), channel_id=1, source_target_pairs={{0,248},{8,0},{16,8},{24,16},{32,24},{40,32},{48,40},{56,48},{64,5... | collective-permute-start | bytes 221192 | tf_op jit(solution)/shard_map/while/body/eval_jaxpr/ppermute | solution.py:25
  350.4 9.2 %collective-permute-start.1 = (f32[32,1152]{1,0:T(8,128)}, f32[32,1152]{1,0:T(8,128)S(1)}, u32[]{:S(2)}, u32[]{:S(2)}) collective-permute-start(f32[32,1152]{1,0:T(8,128)} %convolution_add_fusion.4), channel_id=1, source_target_pairs={{0,248},{8,0},{16,8},{24,16},{32,24},{40,32},{48,40},{56,48},{64,5... | collective-permute-start | bytes 442376 | tf_op jit(solution)/shard_map/while/body/eval_jaxpr/ppermute | solution.py:25
  353.1 6.4 %collective-permute-start = (bf16[32,1152]{1,0:T(8,128)(2,1)S(1)}, bf16[32,1152]{1,0:T(8,128)(2,1)S(1)}, u32[]{:S(2)}, u32[]{:S(2)}) collective-permute-start(bf16[32,1152]{1,0:T(8,128)(2,1)S(1)} %copy.24), channel_id=1, source_target_pairs={{0,248},{8,0},{16,8},{24,16},{32,24},{40,32},{48,40},{56,48},{64,5... | collective-permute-start | bytes 221192 | tf_op jit(solution)/shard_map/while/body/eval_jaxpr/ppermute | solution.py:25
  362.9 9.2 %collective-permute-start.1 = (f32[32,1152]{1,0:T(8,128)}, f32[32,1152]{1,0:T(8,128)S(1)}, u32[]{:S(2)}, u32[]{:S(2)}) collective-permute-start(f32[32,1152]{1,0:T(8,128)} %convolution_add_fusion.4), channel_id=1, source_target_pairs={{0,248},{8,0},{16,8},{24,16},{32,24},{40,32},{48,40},{56,48},{64,5... | collective-permute-start | bytes 442376 | tf_op jit(solution)/shard_map/while/body/eval_jaxpr/ppermute | solution.py:25
  365.6 6.4 %collective-permute-start = (bf16[32,1152]{1,0:T(8,128)(2,1)S(1)}, bf16[32,1152]{1,0:T(8,128)(2,1)S(1)}, u32[]{:S(2)}, u32[]{:S(2)}) collective-permute-start(bf16[32,1152]{1,0:T(8,128)(2,1)S(1)} %copy.24), channel_id=1, source_target_pairs={{0,248},{8,0},{16,8},{24,16},{32,24},{40,32},{48,40},{56,48},{64,5... | collective-permute-start | bytes 221192 | tf_op jit(solution)/shard_map/while/body/eval_jaxpr/ppermute | solution.py:25
  375.4 9.2 %collective-permute-start.1 = (f32[32,1152]{1,0:T(8,128)}, f32[32,1152]{1,0:T(8,128)S(1)}, u32[]{:S(2)}, u32[]{:S(2)}) collective-permute-start(f32[32,1152]{1,0:T(8,128)} %convolution_add_fusion.4), channel_id=1, source_target_pairs={{0,248},{8,0},{16,8},{24,16},{32,24},{40,32},{48,40},{56,48},{64,5... | collective-permute-start | bytes 442376 | tf_op jit(solution)/shard_map/while/body/eval_jaxpr/ppermute | solution.py:25
  378.1 6.4 %collective-permute-start = (bf16[32,1152]{1,0:T(8,128)(2,1)S(1)}, bf16[32,1152]{1,0:T(8,128)(2,1)S(1)}, u32[]{:S(2)}, u32[]{:S(2)}) collective-permute-start(bf16[32,1152]{1,0:T(8,128)(2,1)S(1)} %copy.24), channel_id=1, source_target_pairs={{0,248},{8,0},{16,8},{24,16},{32,24},{40,32},{48,40},{56,48},{64,5... | collective-permute-start | bytes 221192 | tf_op jit(solution)/shard_map/while/body/eval_jaxpr/ppermute | solution.py:25
  387.9 9.2 %collective-permute-start.1 = (f32[32,1152]{1,0:T(8,128)}, f32[32,1152]{1,0:T(8,128)S(1)}, u32[]{:S(2)}, u32[]{:S(2)}) collective-permute-start(f32[32,1152]{1,0:T(8,128)} %convolution_add_fusion.4), channel_id=1, source_target_pairs={{0,248},{8,0},{16,8},{24,16},{32,24},{40,32},{48,40},{56,48},{64,5... | collective-permute-start | bytes 442376 | tf_op jit(solution)/shard_map/while/body/eval_jaxpr/ppermute | solution.py:25
  390.6 6.4 %collective-permute-start = (bf16[32,1152]{1,0:T(8,128)(2,1)S(1)}, bf16[32,1152]{1,0:T(8,128)(2,1)S(1)}, u32[]{:S(2)}, u32[]{:S(2)}) collective-permute-start(bf16[32,1152]{1,0:T(8,128)(2,1)S(1)} %copy.24), channel_id=1, source_target_pairs={{0,248},{8,0},{16,8},{24,16},{32,24},{40,32},{48,40},{56,48},{64,5... | collective-permute-start | bytes 221192 | tf_op jit(solution)/shard_map/while/body/eval_jaxpr/ppermute | solution.py:25
  400.3 9.2 %collective-permute-start.1 = (f32[32,1152]{1,0:T(8,128)}, f32[32,1152]{1,0:T(8,128)S(1)}, u32[]{:S(2)}, u32[]{:S(2)}) collective-permute-start(f32[32,1152]{1,0:T(8,128)} %convolution_add_fusion.4), channel_id=1, source_target_pairs={{0,248},{8,0},{16,8},{24,16},{32,24},{40,32},{48,40},{56,48},{64,5... | collective-permute-start | bytes 442376 | tf_op jit(solution)/shard_map/while/body/eval_jaxpr/ppermute | solution.py:25
  403.1 6.4 %collective-permute-start = (bf16[32,1152]{1,0:T(8,128)(2,1)S(1)}, bf16[32,1152]{1,0:T(8,128)(2,1)S(1)}, u32[]{:S(2)}, u32[]{:S(2)}) collective-permute-start(bf16[32,1152]{1,0:T(8,128)(2,1)S(1)} %copy.24), channel_id=1, source_target_pairs={{0,248},{8,0},{16,8},{24,16},{32,24},{40,32},{48,40},{56,48},{64,5... | collective-permute-start | bytes 221192 | tf_op jit(solution)/shard_map/while/body/eval_jaxpr/ppermute | solution.py:25
  412.8 9.2 %collective-permute-start.1 = (f32[32,1152]{1,0:T(8,128)}, f32[32,1152]{1,0:T(8,128)S(1)}, u32[]{:S(2)}, u32[]{:S(2)}) collective-permute-start(f32[32,1152]{1,0:T(8,128)} %convolution_add_fusion.4), channel_id=1, source_target_pairs={{0,248},{8,0},{16,8},{24,16},{32,24},{40,32},{48,40},{56,48},{64,5... | collective-permute-start | bytes 442376 | tf_op jit(solution)/shard_map/while/body/eval_jaxpr/ppermute | solution.py:25
  424.0 10.6 %collective-permute-start.2 = (f32[32,1152]{1,0:T(8,128)}, f32[32,1152]{1,0:T(8,128)S(1)}, u32[]{:S(2)}, u32[]{:S(2)}) collective-permute-start(f32[32,1152]{1,0:T(8,128)} %convolution_add_fusion.1), channel_id=1, source_target_pairs={{0,88},{8,96},{16,104},{24,112},{32,120},{40,128},{48,136},{56,144... | collective-permute-start | bytes 442376 | tf_op jit(solution)/shard_map/ppermute | solution.py:25
  (13 other events, 755.6 us)
Sparse Core Ops, SparseCore 0:
  9.1 113.3 all-gather.4
  124.3 108.5 all-gather.6
where the time goes:
time: 444 us; the launch traced here: 442 us
  waiting for transfers between devices  242 us (55%)
  starting transfers between devices  91.3 us (21%)
  matrix products  62 us (14%)
  local copies, waits for them, and re-layouts  25 us (6%)
  between operations  14.8 us (3%)
  other arithmetic  7.29 us (2%)
    all_gather x1, waiting for transfers between devices, on_device(): lax.all_gather(fc1_weight, 'fsdp', axis=1, tiled=True)  111 us
    all_gather x1, waiting for transfers between devices, on_device(): lax.all_gather(fc2_weight, 'fsdp', axis=0, tiled=True)  98.5 us
    ppermute x23, starting transfers between devices, from_behind(): lax.ppermute(array, axis, [(i, (i + by) % count) for i in range(count)])  87.7 us
    dot_general x12, matrix products, pair_term(): lax.dot_general(weight, units, (((0,), (0,)), ((), ())), preferred_elemen...  38.2 us
    unnamed x24, local copies, waits for them, and re-layouts  23.9 us
    dot_general x1, matrix products, on_device(): jnp.dot(act, lax.all_gather(fc2_weight, 'fsdp', axis=0, tiled=True), pref...  23.1 us
    ppermute x23, waiting for transfers between devices, from_behind(): lax.ppermute(array, axis, [(i, (i + by) % count) for i in range(count)])  21.2 us
    all_to_all x1, waiting for transfers between devices, from_everyone(): return lax.all_to_all(copies, axis, split_axis=0, concat_axis=0, tiled=True)  9.5 us
  transfers between devices with their start and end apart: 26, of which 15 were waited for; matrix products, arithmetic and copies ran while one was open for 3% of the time, Pallas kernels for 0%

commit v1 on v0

--- a/solution.py
+++ b/solution.py
@@ -63,11 +63,17 @@
         + fc1_bias
     )
     act = jax.nn.gelu(pre, approximate=True).astype(jnp.bfloat16)
-    mixed = jnp.dot(
-        act,
-        lax.all_gather(fc2_weight, "fsdp", axis=0, tiled=True),
-        preferred_element_type=jnp.float32,
-    )
+
+    def _press_hubs(q_in):
+        s_next = jnp.concatenate(
+            lax.all_to_all(
+                jnp.stack([q_in for _ in range(lax.axis_size("fsdp"))], axis=0), "fsdp", 0, 0
+            ),
+            axis=0,
+        )
+        return s_next
+
+    mixed = jnp.dot(act, _press_hubs(fc2_weight), preferred_element_type=jnp.float32)
     out = flat + mixed + fc2_bias
     final = layer_norm(out, final_gain, final_bias).reshape(texts_here, seq_len, width)
     keep = (text_ids != 0).astype(jnp.float32)

time: 444 us -> 481 us (1.083)
  waiting for transfers between devices: 242 us -> 259 us
  starting transfers between devices: 91.3 us -> 105 us
  local copies, waits for them, and re-layouts: 25 us -> 30.8 us
    all_to_all x0 -> x1, waiting for transfers between devices: none -> 170 us  [_press_hubs(): lax.all_to_all(jnp.stack([q_in for _ in range(lax.axis_size('fsdp'))], ax...]
    all_gather x1 -> x0, waiting for transfers between devices: 98.5 us -> none  [on_device(): lax.all_gather(fc2_weight, 'fsdp', axis=0, tiled=True)]
    all_gather x1, waiting for transfers between devices: 111 us -> 58.2 us  [on_device(): lax.all_gather(fc1_weight, 'fsdp', axis=1, tiled=True)]
    unnamed x24 -> x23, local copies, waits for them, and re-layouts: 23.9 us -> 12.1 us
    reshape x0 -> x1, local copies, waits for them, and re-layouts: none -> 11.8 us  [_press_hubs(): jnp.concatenate(lax.all_to_all(jnp.stack([q_in for _ in range(lax.axis_si...]
    all_to_all x0 -> x1, starting transfers between devices: none -> 5.98 us  [_press_hubs(): lax.all_to_all(jnp.stack([q_in for _ in range(lax.axis_size('fsdp'))], ax...]
    another operation x11 -> x12, local copies, waits for them, and re-layouts: 0.07 us -> 5.92 us  [the longest x1 5.85 us: _press_hubs(): jnp.stack([q_in for _ in range(lax.axis_size('fsdp'))], axis=0)]
    ppermute x23, starting transfers between devices: 87.7 us -> 93.1 us  [from_behind(): lax.ppermute(array, axis, [(i, (i + by) % count) for i in range(count)])]
  transfers between devices with their start and end apart: 26 -> 26, of which waited for: 15 -> 15; matrix products, arithmetic and copies ran while one was open for 3% -> 4% of each run, Pallas kernels for 0% -> 0%
where the time goes in v1:
time: 481 us; the launch traced here: 479 us
  waiting for transfers between devices  259 us (54%)
  starting transfers between devices  105 us (22%)
  matrix products  62 us (13%)
  local copies, waits for them, and re-layouts  30.8 us (6%)
  between operations  14.8 us (3%)
  other arithmetic  7.29 us (2%)
    all_to_all x1, waiting for transfers between devices, _press_hubs(): lax.all_to_all(jnp.stack([q_in for _ in range(lax.axis_size('fsdp'))], ax...  170 us
    ppermute x23, starting transfers between devices, from_behind(): lax.ppermute(array, axis, [(i, (i + by) % count) for i in range(count)])  93.1 us
    all_gather x1, waiting for transfers between devices, on_device(): lax.all_gather(fc1_weight, 'fsdp', axis=1, tiled=True)  58.2 us
    dot_general x12, matrix products, pair_term(): lax.dot_general(weight, units, (((0,), (0,)), ((), ())), preferred_elemen...  38.2 us
    dot_general x1, matrix products, on_device(): jnp.dot(act, _press_hubs(fc2_weight), preferred_element_type=jnp.float32)  23.1 us
    ppermute x23, waiting for transfers between devices, from_behind(): lax.ppermute(array, axis, [(i, (i + by) % count) for i in range(count)])  20.4 us
    unnamed x23, local copies, waits for them, and re-layouts  12.1 us
    reshape x1, local copies, waits for them, and re-layouts, _press_hubs(): jnp.concatenate(lax.all_to_all(jnp.stack([q_in for _ in range(lax.axis_si...  11.8 us
  transfers between devices with their start and end apart: 26, of which 15 were waited for; matrix products, arithmetic and copies ran while one was open for 4% of the time, Pallas kernels for 0%

profile of v1, /device:TPU:1, one launch (start us, length us, event | category | flops | bytes accessed | tf_op | source)
XLA Modules:
  0.0 479.0 jit_solution(11411972320996159858)
XLA Ops:
  7.3 5.8 %stack.2 = bf16[8,538,1152]{2,1,0:T(8,128)(2,1)} broadcast(bf16[538,1152]{1,0:T(8,128)(2,1)} %param.24), dimensions={1,2} | broadcast | bytes 11155968 | tf_op jit(solution)/shard_map/stack | solution.py:70
  13.1 6.0 %all-to-all-start = ((bf16[8,538,1152]{2,1,0:T(8,128)(2,1)}), bf16[8,538,1152]{2,1,0:T(8,128)(2,1)}, u32[]{:S(2)}, u32[]{:S(2)}) async-start(bf16[8,538,1152]{2,1,0:T(8,128)(2,1)} %stack.2), calls=%async_computation | async-start | bytes 20054016 | tf_op jit(solution)/shard_map/all_to_all | solution.py:69
  22.6 170.2 %all-to-all-done = bf16[8,538,1152]{2,1,0:T(8,128)(2,1)} async-done(((bf16[8,538,1152]{2,1,0:T(8,128)(2,1)}), bf16[8,538,1152]{2,1,0:T(8,128)(2,1)}, u32[]{:S(2)}, u32[]{:S(2)}) %all-to-all-start) | async-done | bytes 9916448 | tf_op jit(solution)/shard_map/all_to_all | solution.py:69
  192.7 11.8 %reshape.66 = bf16[4304,1152]{1,0:T(8,128)(2,1)} reshape(bf16[8,538,1152]{2,1,0:T(8,128)(2,1)} %all-to-all-done) | data formatting | bytes 19832832 | tf_op jit(solution)/shard_map/reshape | solution.py:68
  204.6 58.2 %all-gather.3.cloned.1.call-done = bf16[8,538,1152]{2,1,0:T(8,128)(2,1)} async-done(((bf16[1,538,1152]{2,1,0:T(8,128)(2,1)}), bf16[8,538,1152]{2,1,0:T(8,128)(2,1)}) %all-gather.3.cloned.1.call-update) | async-done | bytes 9916432 | tf_op jit(solution)/shard_map/all_gather | solution.py:60
  262.7 11.9 %reshape.74 = bf16[4304,1152]{1,0:T(8,128)(2,1)} reshape(bf16[8,538,1152]{2,1,0:T(8,128)(2,1)} %all-gather.3.cloned.1.call-done) | data formatting | bytes 19832832
  274.7 23.1 %fusion.72 = (f32[512]{0:T(512)S(1)}, f32[512,1152]{1,0:T(8,128)}) fusion(f32[1152]{0:T(1024)S(1)} %copy-done.8, bf16[4304,1152]{1,0:T(8,128)(2,1)} %reshape.66, bf16[4304,1152]{1,0:T(8,128)(2,1)} %reshape.74, f32[4304]{0:T(1024)S(1)} %copy-done.7, bf16[512,1152]{1,0:T(8,128)(2,1)} %param.18, f32[1152]{0:T(1024)S(1)} %copy-done.9, f32[1152]{0:T(1024)S(1)} %copy-done.10, ...), kind=kOutput, calls=%fused_computation.91 | convolution fusion | flops 10182344704 | bytes 23408960 | tf_op jit(solution)/shard_map/dot_general | solution.py:76
  302.7 5.9 %all-to-all-start.1 = ((bf16[8,32,1152]{2,1,0:T(8,128)(2,1)}), bf16[8,32,1152]{2,1,0:T(8,128)(2,1)S(1)}, u32[]{:S(2)}, u32[]{:S(2)}) async-start(bf16[8,32,1152]{2,1,0:T(8,128)(2,1)} %broadcast_in_dim.5), calls=%async_computation.1 | async-start | bytes 1179648 | tf_op jit(solution)/shard_map/all_to_all | solution.py:9
  310.1 9.6 %all-to-all-done.1 = bf16[8,32,1152]{2,1,0:T(8,128)(2,1)S(1)} async-done(((bf16[8,32,1152]{2,1,0:T(8,128)(2,1)}), bf16[8,32,1152]{2,1,0:T(8,128)(2,1)S(1)}, u32[]{:S(2)}, u32[]{:S(2)}) %all-to-all-start.1) | async-done | bytes 589856 | tf_op jit(solution)/shard_map/all_to_all | solution.py:9
  319.6 139.5 %while.15 = (s32[]{:T(128)}, bf16[32,1152]{1,0:T(8,128)(2,1)S(1)}, f32[32,1152]{1,0:T(8,128)S(1)}, f32[]{:T(128)}, bf16[256,1152]{1,0:T(8,128)(2,1)S(1)}, /*inde...) while((s32[]{:T(128)}, bf16[32,1152]{1,0:T(8,128)(2,1)S(1)}, f32[32,1152]{1,0:T(8,128)S(1)}, f32[]{:T(128)}, ...), condition=%wide.region_9.10_spmd, body=%wide.region_8.9_spmd.sunk | while | flops 37875712 | bytes 2598565 | solution.py:123
  319.7 3.3 convolution_add_fusion.4
  323.7 9.6 %collective-permute-start = (bf16[32,1152]{1,0:T(8,128)(2,1)S(1)}, bf16[32,1152]{1,0:T(8,128)(2,1)S(1)}, u32[]{:S(2)}, u32[]{:S(2)}) collective-permute-start(bf16[32,1152]{1,0:T(8,128)(2,1)S(1)} %copy.24), channel_id=1, source_target_pairs={{0,248},{8,0},{16,8},{24,16},{32,24},{40,32},{48,40},{56,48},{64,5... | collective-permute-start | bytes 221192 | tf_op jit(solution)/shard_map/while/body/eval_jaxpr/ppermute | solution.py:25
  334.3 3.3 convolution_add_fusion.4
  340.3 5.5 %collective-permute-start = (bf16[32,1152]{1,0:T(8,128)(2,1)S(1)}, bf16[32,1152]{1,0:T(8,128)(2,1)S(1)}, u32[]{:S(2)}, u32[]{:S(2)}) collective-permute-start(bf16[32,1152]{1,0:T(8,128)(2,1)S(1)} %copy.24), channel_id=1, source_target_pairs={{0,248},{8,0},{16,8},{24,16},{32,24},{40,32},{48,40},{56,48},{64,5... | collective-permute-start | bytes 221192 | tf_op jit(solution)/shard_map/while/body/eval_jaxpr/ppermute | solution.py:25
  352.8 5.5 %collective-permute-start = (bf16[32,1152]{1,0:T(8,128)(2,1)S(1)}, bf16[32,1152]{1,0:T(8,128)(2,1)S(1)}, u32[]{:S(2)}, u32[]{:S(2)}) collective-permute-start(bf16[32,1152]{1,0:T(8,128)(2,1)S(1)} %copy.24), channel_id=1, source_target_pairs={{0,248},{8,0},{16,8},{24,16},{32,24},{40,32},{48,40},{56,48},{64,5... | collective-permute-start | bytes 221192 | tf_op jit(solution)/shard_map/while/body/eval_jaxpr/ppermute | solution.py:25
  365.3 5.5 %collective-permute-start = (bf16[32,1152]{1,0:T(8,128)(2,1)S(1)}, bf16[32,1152]{1,0:T(8,128)(2,1)S(1)}, u32[]{:S(2)}, u32[]{:S(2)}) collective-permute-start(bf16[32,1152]{1,0:T(8,128)(2,1)S(1)} %copy.24), channel_id=1, source_target_pairs={{0,248},{8,0},{16,8},{24,16},{32,24},{40,32},{48,40},{56,48},{64,5... | collective-permute-start | bytes 221192 | tf_op jit(solution)/shard_map/while/body/eval_jaxpr/ppermute | solution.py:25
  377.8 5.5 %collective-permute-start = (bf16[32,1152]{1,0:T(8,128)(2,1)S(1)}, bf16[32,1152]{1,0:T(8,128)(2,1)S(1)}, u32[]{:S(2)}, u32[]{:S(2)}) collective-permute-start(bf16[32,1152]{1,0:T(8,128)(2,1)S(1)} %copy.24), channel_id=1, source_target_pairs={{0,248},{8,0},{16,8},{24,16},{32,24},{40,32},{48,40},{56,48},{64,5... | collective-permute-start | bytes 221192 | tf_op jit(solution)/shard_map/while/body/eval_jaxpr/ppermute | solution.py:25
  390.3 5.5 %collective-permute-start = (bf16[32,1152]{1,0:T(8,128)(2,1)S(1)}, bf16[32,1152]{1,0:T(8,128)(2,1)S(1)}, u32[]{:S(2)}, u32[]{:S(2)}) collective-permute-start(bf16[32,1152]{1,0:T(8,128)(2,1)S(1)} %copy.24), channel_id=1, source_target_pairs={{0,248},{8,0},{16,8},{24,16},{32,24},{40,32},{48,40},{56,48},{64,5... | collective-permute-start | bytes 221192 | tf_op jit(solution)/shard_map/while/body/eval_jaxpr/ppermute | solution.py:25
  402.8 5.5 %collective-permute-start = (bf16[32,1152]{1,0:T(8,128)(2,1)S(1)}, bf16[32,1152]{1,0:T(8,128)(2,1)S(1)}, u32[]{:S(2)}, u32[]{:S(2)}) collective-permute-start(bf16[32,1152]{1,0:T(8,128)(2,1)S(1)} %copy.24), channel_id=1, source_target_pairs={{0,248},{8,0},{16,8},{24,16},{32,24},{40,32},{48,40},{56,48},{64,5... | collective-permute-start | bytes 221192 | tf_op jit(solution)/shard_map/while/body/eval_jaxpr/ppermute | solution.py:25
  415.3 5.5 %collective-permute-start = (bf16[32,1152]{1,0:T(8,128)(2,1)S(1)}, bf16[32,1152]{1,0:T(8,128)(2,1)S(1)}, u32[]{:S(2)}, u32[]{:S(2)}) collective-permute-start(bf16[32,1152]{1,0:T(8,128)(2,1)S(1)} %copy.24), channel_id=1, source_target_pairs={{0,248},{8,0},{16,8},{24,16},{32,24},{40,32},{48,40},{56,48},{64,5... | collective-permute-start | bytes 221192 | tf_op jit(solution)/shard_map/while/body/eval_jaxpr/ppermute | solution.py:25
  427.7 5.5 %collective-permute-start = (bf16[32,1152]{1,0:T(8,128)(2,1)S(1)}, bf16[32,1152]{1,0:T(8,128)(2,1)S(1)}, u32[]{:S(2)}, u32[]{:S(2)}) collective-permute-start(bf16[32,1152]{1,0:T(8,128)(2,1)S(1)} %copy.24), channel_id=1, source_target_pairs={{0,248},{8,0},{16,8},{24,16},{32,24},{40,32},{48,40},{56,48},{64,5... | collective-permute-start | bytes 221192 | tf_op jit(solution)/shard_map/while/body/eval_jaxpr/ppermute | solution.py:25
  440.2 5.5 %collective-permute-start = (bf16[32,1152]{1,0:T(8,128)(2,1)S(1)}, bf16[32,1152]{1,0:T(8,128)(2,1)S(1)}, u32[]{:S(2)}, u32[]{:S(2)}) collective-permute-start(bf16[32,1152]{1,0:T(8,128)(2,1)S(1)} %copy.24), channel_id=1, source_target_pairs={{0,248},{8,0},{16,8},{24,16},{32,24},{40,32},{48,40},{56,48},{64,5... | collective-permute-start | bytes 221192 | tf_op jit(solution)/shard_map/while/body/eval_jaxpr/ppermute | solution.py:25
  452.7 5.5 %collective-permute-start = (bf16[32,1152]{1,0:T(8,128)(2,1)S(1)}, bf16[32,1152]{1,0:T(8,128)(2,1)S(1)}, u32[]{:S(2)}, u32[]{:S(2)}) collective-permute-start(bf16[32,1152]{1,0:T(8,128)(2,1)S(1)} %copy.24), channel_id=1, source_target_pairs={{0,248},{8,0},{16,8},{24,16},{32,24},{40,32},{48,40},{56,48},{64,5... | collective-permute-start | bytes 221192 | tf_op jit(solution)/shard_map/while/body/eval_jaxpr/ppermute | solution.py:25
  461.1 10.3 %collective-permute-done.2 = f32[32,1152]{1,0:T(8,128)S(1)} collective-permute-done((f32[32,1152]{1,0:T(8,128)}, f32[32,1152]{1,0:T(8,128)S(1)}, u32[]{:S(2)}, u32[]{:S(2)}) %collective-permute-start.2) | collective-permute-done | bytes 147488 | tf_op jit(solution)/shard_map/ppermute | solution.py:25
  (99 shorter events, 79.9 us)
Async XLA Ops:
  6.5 256.2 %all-gather.3.cloned.1.call-start = ((), (), s32[]{:S(2)}) async-start(), calls=%async_computation.2 | async-start | bytes 11280384 | tf_op jit(solution)/shard_map/all_gather | solution.py:60
  13.1 179.6 %all-to-all-start = ((bf16[8,538,1152]{2,1,0:T(8,128)(2,1)}), bf16[8,538,1152]{2,1,0:T(8,128)(2,1)}, u32[]{:S(2)}, u32[]{:S(2)}) async-start(bf16[8,538,1152]{2,1,0:T(8,128)(2,1)} %stack.2), calls=%async_computation | async-start | bytes 20054016 | tf_op jit(solution)/shard_map/all_to_all | solution.py:69
  302.7 16.9 %all-to-all-start.1 = ((bf16[8,32,1152]{2,1,0:T(8,128)(2,1)}), bf16[8,32,1152]{2,1,0:T(8,128)(2,1)S(1)}, u32[]{:S(2)}, u32[]{:S(2)}) async-start(bf16[8,32,1152]{2,1,0:T(8,128)(2,1)} %broadcast_in_dim.5), calls=%async_computation.1 | async-start | bytes 1179648 | tf_op jit(solution)/shard_map/all_to_all | solution.py:9
  322.9 11.4 %collective-permute-start.1 = (f32[32,1152]{1,0:T(8,128)}, f32[32,1152]{1,0:T(8,128)S(1)}, u32[]{:S(2)}, u32[]{:S(2)}) collective-permute-start(f32[32,1152]{1,0:T(8,128)} %convolution_add_fusion.4), channel_id=1, source_target_pairs={{0,248},{8,0},{16,8},{24,16},{32,24},{40,32},{48,40},{56,48},{64,5... | collective-permute-start | bytes 442376 | tf_op jit(solution)/shard_map/while/body/eval_jaxpr/ppermute | solution.py:25
  323.7 10.6 %collective-permute-start = (bf16[32,1152]{1,0:T(8,128)(2,1)S(1)}, bf16[32,1152]{1,0:T(8,128)(2,1)S(1)}, u32[]{:S(2)}, u32[]{:S(2)}) collective-permute-start(bf16[32,1152]{1,0:T(8,128)(2,1)S(1)} %copy.24), channel_id=1, source_target_pairs={{0,248},{8,0},{16,8},{24,16},{32,24},{40,32},{48,40},{56,48},{64,5... | collective-permute-start | bytes 221192 | tf_op jit(solution)/shard_map/while/body/eval_jaxpr/ppermute | solution.py:25
  337.6 9.2 %collective-permute-start.1 = (f32[32,1152]{1,0:T(8,128)}, f32[32,1152]{1,0:T(8,128)S(1)}, u32[]{:S(2)}, u32[]{:S(2)}) collective-permute-start(f32[32,1152]{1,0:T(8,128)} %convolution_add_fusion.4), channel_id=1, source_target_pairs={{0,248},{8,0},{16,8},{24,16},{32,24},{40,32},{48,40},{56,48},{64,5... | collective-permute-start | bytes 442376 | tf_op jit(solution)/shard_map/while/body/eval_jaxpr/ppermute | solution.py:25
  340.3 6.4 %collective-permute-start = (bf16[32,1152]{1,0:T(8,128)(2,1)S(1)}, bf16[32,1152]{1,0:T(8,128)(2,1)S(1)}, u32[]{:S(2)}, u32[]{:S(2)}) collective-permute-start(bf16[32,1152]{1,0:T(8,128)(2,1)S(1)} %copy.24), channel_id=1, source_target_pairs={{0,248},{8,0},{16,8},{24,16},{32,24},{40,32},{48,40},{56,48},{64,5... | collective-permute-start | bytes 221192 | tf_op jit(solution)/shard_map/while/body/eval_jaxpr/ppermute | solution.py:25
  350.1 9.2 %collective-permute-start.1 = (f32[32,1152]{1,0:T(8,128)}, f32[32,1152]{1,0:T(8,128)S(1)}, u32[]{:S(2)}, u32[]{:S(2)}) collective-permute-start(f32[32,1152]{1,0:T(8,128)} %convolution_add_fusion.4), channel_id=1, source_target_pairs={{0,248},{8,0},{16,8},{24,16},{32,24},{40,32},{48,40},{56,48},{64,5... | collective-permute-start | bytes 442376 | tf_op jit(solution)/shard_map/while/body/eval_jaxpr/ppermute | solution.py:25
  352.8 6.4 %collective-permute-start = (bf16[32,1152]{1,0:T(8,128)(2,1)S(1)}, bf16[32,1152]{1,0:T(8,128)(2,1)S(1)}, u32[]{:S(2)}, u32[]{:S(2)}) collective-permute-start(bf16[32,1152]{1,0:T(8,128)(2,1)S(1)} %copy.24), channel_id=1, source_target_pairs={{0,248},{8,0},{16,8},{24,16},{32,24},{40,32},{48,40},{56,48},{64,5... | collective-permute-start | bytes 221192 | tf_op jit(solution)/shard_map/while/body/eval_jaxpr/ppermute | solution.py:25
  362.6 9.2 %collective-permute-start.1 = (f32[32,1152]{1,0:T(8,128)}, f32[32,1152]{1,0:T(8,128)S(1)}, u32[]{:S(2)}, u32[]{:S(2)}) collective-permute-start(f32[32,1152]{1,0:T(8,128)} %convolution_add_fusion.4), channel_id=1, source_target_pairs={{0,248},{8,0},{16,8},{24,16},{32,24},{40,32},{48,40},{56,48},{64,5... | collective-permute-start | bytes 442376 | tf_op jit(solution)/shard_map/while/body/eval_jaxpr/ppermute | solution.py:25
  365.3 6.4 %collective-permute-start = (bf16[32,1152]{1,0:T(8,128)(2,1)S(1)}, bf16[32,1152]{1,0:T(8,128)(2,1)S(1)}, u32[]{:S(2)}, u32[]{:S(2)}) collective-permute-start(bf16[32,1152]{1,0:T(8,128)(2,1)S(1)} %copy.24), channel_id=1, source_target_pairs={{0,248},{8,0},{16,8},{24,16},{32,24},{40,32},{48,40},{56,48},{64,5... | collective-permute-start | bytes 221192 | tf_op jit(solution)/shard_map/while/body/eval_jaxpr/ppermute | solution.py:25
  375.0 9.2 %collective-permute-start.1 = (f32[32,1152]{1,0:T(8,128)}, f32[32,1152]{1,0:T(8,128)S(1)}, u32[]{:S(2)}, u32[]{:S(2)}) collective-permute-start(f32[32,1152]{1,0:T(8,128)} %convolution_add_fusion.4), channel_id=1, source_target_pairs={{0,248},{8,0},{16,8},{24,16},{32,24},{40,32},{48,40},{56,48},{64,5... | collective-permute-start | bytes 442376 | tf_op jit(solution)/shard_map/while/body/eval_jaxpr/ppermute | solution.py:25
  377.8 6.4 %collective-permute-start = (bf16[32,1152]{1,0:T(8,128)(2,1)S(1)}, bf16[32,1152]{1,0:T(8,128)(2,1)S(1)}, u32[]{:S(2)}, u32[]{:S(2)}) collective-permute-start(bf16[32,1152]{1,0:T(8,128)(2,1)S(1)} %copy.24), channel_id=1, source_target_pairs={{0,248},{8,0},{16,8},{24,16},{32,24},{40,32},{48,40},{56,48},{64,5... | collective-permute-start | bytes 221192 | tf_op jit(solution)/shard_map/while/body/eval_jaxpr/ppermute | solution.py:25
  387.5 9.2 %collective-permute-start.1 = (f32[32,1152]{1,0:T(8,128)}, f32[32,1152]{1,0:T(8,128)S(1)}, u32[]{:S(2)}, u32[]{:S(2)}) collective-permute-start(f32[32,1152]{1,0:T(8,128)} %convolution_add_fusion.4), channel_id=1, source_target_pairs={{0,248},{8,0},{16,8},{24,16},{32,24},{40,32},{48,40},{56,48},{64,5... | collective-permute-start | bytes 442376 | tf_op jit(solution)/shard_map/while/body/eval_jaxpr/ppermute | solution.py:25
  390.3 6.4 %collective-permute-start = (bf16[32,1152]{1,0:T(8,128)(2,1)S(1)}, bf16[32,1152]{1,0:T(8,128)(2,1)S(1)}, u32[]{:S(2)}, u32[]{:S(2)}) collective-permute-start(bf16[32,1152]{1,0:T(8,128)(2,1)S(1)} %copy.24), channel_id=1, source_target_pairs={{0,248},{8,0},{16,8},{24,16},{32,24},{40,32},{48,40},{56,48},{64,5... | collective-permute-start | bytes 221192 | tf_op jit(solution)/shard_map/while/body/eval_jaxpr/ppermute | solution.py:25
  400.0 9.2 %collective-permute-start.1 = (f32[32,1152]{1,0:T(8,128)}, f32[32,1152]{1,0:T(8,128)S(1)}, u32[]{:S(2)}, u32[]{:S(2)}) collective-permute-start(f32[32,1152]{1,0:T(8,128)} %convolution_add_fusion.4), channel_id=1, source_target_pairs={{0,248},{8,0},{16,8},{24,16},{32,24},{40,32},{48,40},{56,48},{64,5... | collective-permute-start | bytes 442376 | tf_op jit(solution)/shard_map/while/body/eval_jaxpr/ppermute | solution.py:25
  402.8 6.4 %collective-permute-start = (bf16[32,1152]{1,0:T(8,128)(2,1)S(1)}, bf16[32,1152]{1,0:T(8,128)(2,1)S(1)}, u32[]{:S(2)}, u32[]{:S(2)}) collective-permute-start(bf16[32,1152]{1,0:T(8,128)(2,1)S(1)} %copy.24), channel_id=1, source_target_pairs={{0,248},{8,0},{16,8},{24,16},{32,24},{40,32},{48,40},{56,48},{64,5... | collective-permute-start | bytes 221192 | tf_op jit(solution)/shard_map/while/body/eval_jaxpr/ppermute | solution.py:25
  412.5 9.2 %collective-permute-start.1 = (f32[32,1152]{1,0:T(8,128)}, f32[32,1152]{1,0:T(8,128)S(1)}, u32[]{:S(2)}, u32[]{:S(2)}) collective-permute-start(f32[32,1152]{1,0:T(8,128)} %convolution_add_fusion.4), channel_id=1, source_target_pairs={{0,248},{8,0},{16,8},{24,16},{32,24},{40,32},{48,40},{56,48},{64,5... | collective-permute-start | bytes 442376 | tf_op jit(solution)/shard_map/while/body/eval_jaxpr/ppermute | solution.py:25
  415.3 6.4 %collective-permute-start = (bf16[32,1152]{1,0:T(8,128)(2,1)S(1)}, bf16[32,1152]{1,0:T(8,128)(2,1)S(1)}, u32[]{:S(2)}, u32[]{:S(2)}) collective-permute-start(bf16[32,1152]{1,0:T(8,128)(2,1)S(1)} %copy.24), channel_id=1, source_target_pairs={{0,248},{8,0},{16,8},{24,16},{32,24},{40,32},{48,40},{56,48},{64,5... | collective-permute-start | bytes 221192 | tf_op jit(solution)/shard_map/while/body/eval_jaxpr/ppermute | solution.py:25
  425.0 9.2 %collective-permute-start.1 = (f32[32,1152]{1,0:T(8,128)}, f32[32,1152]{1,0:T(8,128)S(1)}, u32[]{:S(2)}, u32[]{:S(2)}) collective-permute-start(f32[32,1152]{1,0:T(8,128)} %convolution_add_fusion.4), channel_id=1, source_target_pairs={{0,248},{8,0},{16,8},{24,16},{32,24},{40,32},{48,40},{56,48},{64,5... | collective-permute-start | bytes 442376 | tf_op jit(solution)/shard_map/while/body/eval_jaxpr/ppermute | solution.py:25
  427.7 6.4 %collective-permute-start = (bf16[32,1152]{1,0:T(8,128)(2,1)S(1)}, bf16[32,1152]{1,0:T(8,128)(2,1)S(1)}, u32[]{:S(2)}, u32[]{:S(2)}) collective-permute-start(bf16[32,1152]{1,0:T(8,128)(2,1)S(1)} %copy.24), channel_id=1, source_target_pairs={{0,248},{8,0},{16,8},{24,16},{32,24},{40,32},{48,40},{56,48},{64,5... | collective-permute-start | bytes 221192 | tf_op jit(solution)/shard_map/while/body/eval_jaxpr/ppermute | solution.py:25
  437.5 9.2 %collective-permute-start.1 = (f32[32,1152]{1,0:T(8,128)}, f32[32,1152]{1,0:T(8,128)S(1)}, u32[]{:S(2)}, u32[]{:S(2)}) collective-permute-start(f32[32,1152]{1,0:T(8,128)} %convolution_add_fusion.4), channel_id=1, source_target_pairs={{0,248},{8,0},{16,8},{24,16},{32,24},{40,32},{48,40},{56,48},{64,5... | collective-permute-start | bytes 442376 | tf_op jit(solution)/shard_map/while/body/eval_jaxpr/ppermute | solution.py:25
  450.0 9.2 %collective-permute-start.1 = (f32[32,1152]{1,0:T(8,128)}, f32[32,1152]{1,0:T(8,128)S(1)}, u32[]{:S(2)}, u32[]{:S(2)}) collective-permute-start(f32[32,1152]{1,0:T(8,128)} %convolution_add_fusion.4), channel_id=1, source_target_pairs={{0,248},{8,0},{16,8},{24,16},{32,24},{40,32},{48,40},{56,48},{64,5... | collective-permute-start | bytes 442376 | tf_op jit(solution)/shard_map/while/body/eval_jaxpr/ppermute | solution.py:25
  461.1 10.3 %collective-permute-start.2 = (f32[32,1152]{1,0:T(8,128)}, f32[32,1152]{1,0:T(8,128)S(1)}, u32[]{:S(2)}, u32[]{:S(2)}) collective-permute-start(f32[32,1152]{1,0:T(8,128)} %convolution_add_fusion.1), channel_id=1, source_target_pairs={{0,88},{8,96},{16,104},{24,112},{32,120},{40,128},{48,136},{56,144... | collective-permute-start | bytes 442376 | tf_op jit(solution)/shard_map/ppermute | solution.py:25
  (13 other events, 633.1 us)
Sparse Core Ops, SparseCore 0:
  9.1 253.5 all-gather.2
